TPU v7x, 32 devices: a whole 2x2x4 slice. The times are simulated.
32 devices in a mesh: prompt: 8 (over y, x, core), seq: 4 (over z).
Axes of the slice: x: 2, y: 2, z: 4, core: 2. Of those that a mesh axis runs over, the one named last changes fastest.
Arguments:
- queries: bfloat16 [8, 512, 4096], P('prompt', 'seq'), may hold values from -8 to 8
- self_keys: bfloat16 [8, 512, 4096], P('prompt', 'seq'), may hold values from -8 to 8
- self_values: bfloat16 [8, 512, 4096], P('prompt', 'seq'), may hold values from -6 to 6
- cross_queries: bfloat16 [8, 512, 4096], P('prompt', 'seq')
- context: bfloat16 [8, 512, 5120], P('prompt', 'seq')
- key_weight: bfloat16 [5120, 4096], P('prompt', 'seq')
- value_weight: bfloat16 [5120, 4096], P('prompt', 'seq'), may hold values from -0.078125 to 0.078125
- lengths: int32 [8], P('prompt'), may hold values from 64 to 512, as said below
Outputs:
- attended: bfloat16 [8, 512, 4096], P('prompt', 'seq')
Inputs may be any that keep to these rules, and one draw needn't show every extreme that they name: `lengths`: each prompt's number of text tokens; some prompt has all 512.
All inputs are finite; a program needn't handle non-finite values.
Results may differ from a plain program's by a relative error of at most 0.007.
Values may be sent and summed in bfloat16 or wider, within the bound.
A program may use at most 128 MiB of HBM per device.

v0:
```python
import math
import jax
import jax.numpy as jnp
from jax import lax
from jax.sharding import PartitionSpec as P

HD = 128


def head_attend(query_rows, key_rows, value_rows, length, head_count):
    scaling = 1.0 / math.sqrt(HD)
    row_count = query_rows.shape[0]
    key_count = key_rows.shape[0]
    query_split = query_rows.reshape(row_count, head_count, HD)
    key_split = key_rows.reshape(key_count, head_count, HD)
    value_split = value_rows.reshape(key_count, head_count, HD)
    scores = (
        jnp.einsum("rhd,lhd->hrl", query_split, key_split, preferred_element_type=jnp.float32)
        * scaling
    )
    if length is None:
        row_max = jnp.max(scores, axis=2)
        weights = jnp.exp(scores - row_max[:, :, None])
    else:
        usable = (jnp.arange(key_count, dtype=jnp.int32) < length)[None, None, :]
        row_max = jnp.max(jnp.where(usable, scores, -jnp.inf), axis=2)
        shifted = jnp.where(usable, scores, row_max[:, :, None]) - row_max[:, :, None]
        weights = jnp.where(usable, jnp.exp(shifted), jnp.zeros_like(shifted))
    totals = jnp.sum(weights, axis=2)
    mixed = jnp.einsum(
        "hrl,lhd->rhd",
        weights.astype(jnp.bfloat16),
        value_split,
        preferred_element_type=jnp.float32,
    )
    return (
        (mixed / jnp.transpose(totals)[:, :, None])
        .reshape(row_count, head_count * HD)
        .astype(jnp.bfloat16)
    )


def by_blocks(function, query_rows):
    row_count = query_rows.shape[0]
    block_rows = math.gcd(row_count, 512)
    stacked = query_rows.reshape(row_count // block_rows, block_rows, query_rows.shape[1])
    return lax.map(function, stacked).reshape(row_count, -1)


def self_attend(query_heads, key_heads, value_heads, head_count):

    def self_run_block(block):
        return head_attend(block, key_heads, value_heads, None, head_count)

    return by_blocks(self_run_block, query_heads)


def cross_attend(query_rows, key_rows, value_rows, length, head_count):

    def cross_run_block(block):
        return head_attend(block, key_rows, value_rows, length, head_count)

    return by_blocks(cross_run_block, query_rows)


def body(
    queries, self_keys, self_values, cross_queries, context, key_weight, value_weight, lengths
):
    query_local = queries[0]
    key_local = self_keys[0]
    value_local = self_values[0]
    cross_local = cross_queries[0]
    length = lengths[0]
    head_local = key_weight.shape[1] // HD
    text_full = lax.all_gather(context[0], "seq", axis=0, tiled=True)
    key_sums = jnp.dot(
        text_full,
        lax.all_gather(key_weight, "prompt", axis=0, tiled=True),
        preferred_element_type=jnp.float32,
    )
    value_sums = jnp.dot(
        text_full,
        lax.all_gather(value_weight, "prompt", axis=0, tiled=True),
        preferred_element_type=jnp.float32,
    )
    text_keys = key_sums.astype(jnp.bfloat16)
    text_values = value_sums.astype(jnp.bfloat16)
    query_heads, key_heads, value_heads, cross_heads = (
        lax.all_to_all(query_local, "seq", split_axis=1, concat_axis=0, tiled=True),
        lax.all_to_all(key_local, "seq", split_axis=1, concat_axis=0, tiled=True),
        lax.all_to_all(value_local, "seq", split_axis=1, concat_axis=0, tiled=True),
        lax.all_to_all(cross_local, "seq", split_axis=1, concat_axis=0, tiled=True),
    )
    self_heads = self_attend(query_heads, key_heads, value_heads, head_local)
    cross_part = cross_attend(cross_heads, text_keys, text_values, length, head_local)
    summed = (self_heads.astype(jnp.float32) + cross_part.astype(jnp.float32)).astype(jnp.bfloat16)
    attended = lax.all_to_all(summed, "seq", split_axis=0, concat_axis=1, tiled=True)
    return attended[None]


def solution(mesh):
    in_specs = (
        P("prompt", "seq", None),
        P("prompt", "seq", None),
        P("prompt", "seq", None),
        P("prompt", "seq", None),
        P("prompt", "seq", None),
        P("prompt", "seq"),
        P("prompt", "seq"),
        P("prompt"),
    )
    out_specs = P("prompt", "seq", None)
    return jax.shard_map(body, mesh=mesh, in_specs=in_specs, out_specs=out_specs, check_vma=False)
```

profile of v0, /device:TPU:0, one launch (start us, length us, event | category | flops | bytes accessed | tf_op | source)
XLA Modules:
  0.0 361.7 jit_solution(14141983873178840253)
XLA Ops:
  6.5 0.0 copy-start.2
  6.5 0.0 all-gather.9.cloned.1.call-start
  6.5 0.7 all-gather.9.cloned.1.call-update
  7.3 0.0 all-gather.5.cloned.1.call-start
  7.3 0.7 all-gather.5.cloned.1.call-update
  8.0 0.0 all-gather.7.cloned.1.call-start
  8.1 0.7 all-gather.7.cloned.1.call-update
  8.7 1.9 all_to_all.58
  10.6 1.3 copy.28
  11.9 6.3 %all-to-all-start = ((bf16[128,4,1024]{2,0,1:T(8,128)(2,1)}), bf16[128,4,1024]{2,0,1:T(8,128)(2,1)S(1)}, u32[]{:S(2)}, u32[]{:S(2)}) async-start(bf16[128,4,1024]{2,0,1:T(8,128)(2,1)} %copy.28), calls=%async_computation | async-start | bytes 2097152 | tf_op jit(solution)/shard_map/all_to_all | solution.py:89
  18.2 0.0 copy-done.2
  18.2 0.8 all_to_all.61
  19.0 1.3 copy.29
  20.3 52.6 %all-to-all-done = bf16[128,4,1024]{2,0,1:T(8,128)(2,1)S(1)} async-done(((bf16[128,4,1024]{2,0,1:T(8,128)(2,1)}), bf16[128,4,1024]{2,0,1:T(8,128)(2,1)S(1)}, u32[]{:S(2)}, u32[]{:S(2)}) %all-to-all-start) | async-done | bytes 1048608 | tf_op jit(solution)/shard_map/all_to_all | solution.py:89
  72.9 3.5 all-to-all-start.1
  76.4 1.9 all_to_all.64
  78.3 1.3 copy.32
  79.6 46.6 %all-to-all-done.1 = bf16[128,4,1024]{2,0,1:T(8,128)(2,1)S(1)} async-done(((bf16[128,4,1024]{2,0,1:T(8,128)(2,1)}), bf16[128,4,1024]{2,0,1:T(8,128)(2,1)S(1)}, u32[]{:S(2)}, u32[]{:S(2)}) %all-to-all-start.1) | async-done | bytes 1048608 | tf_op jit(solution)/shard_map/all_to_all | solution.py:90
  126.2 7.5 %all-to-all-start.2 = ((bf16[128,4,1024]{2,0,1:T(8,128)(2,1)}), bf16[128,4,1024]{2,0,1:T(8,128)(2,1)S(1)}, u32[]{:S(2)}, u32[]{:S(2)}) async-start(bf16[128,4,1024]{2,0,1:T(8,128)(2,1)} %copy.32), calls=%async_computation.2 | async-start | bytes 2097152 | tf_op jit(solution)/shard_map/all_to_all | solution.py:91
  133.7 2.6 all_to_all.67
  136.3 2.5 copy.35
  138.9 32.6 %all-to-all-done.2 = bf16[128,4,1024]{2,0,1:T(8,128)(2,1)S(1)} async-done(((bf16[128,4,1024]{2,0,1:T(8,128)(2,1)}), bf16[128,4,1024]{2,0,1:T(8,128)(2,1)S(1)}, u32[]{:S(2)}, u32[]{:S(2)}) %all-to-all-start.2) | async-done | bytes 1048608 | tf_op jit(solution)/shard_map/all_to_all | solution.py:91
  171.5 0.0 copy-start.1
  171.5 4.4 %all-to-all-start.3 = ((bf16[128,4,1024]{2,0,1:T(8,128)(2,1)}), bf16[128,4,1024]{2,0,1:T(8,128)(2,1)}, u32[]{:S(2)}, u32[]{:S(2)}) async-start(bf16[128,4,1024]{2,0,1:T(8,128)(2,1)} %copy.35), calls=%async_computation.3 | async-start | bytes 2097152 | tf_op jit(solution)/shard_map/all_to_all | solution.py:92
  176.6 0.0 copy-done.1
  176.6 0.3 copy.49
  176.9 0.3 copy.50
  177.2 1.5 copy.51
  178.7 20.3 %all-to-all-done.3 = bf16[128,4,1024]{2,0,1:T(8,128)(2,1)} async-done(((bf16[128,4,1024]{2,0,1:T(8,128)(2,1)}), bf16[128,4,1024]{2,0,1:T(8,128)(2,1)}, u32[]{:S(2)}, u32[]{:S(2)}) %all-to-all-start.3) | async-done | bytes 1048608 | tf_op jit(solution)/shard_map/all_to_all | solution.py:92
  199.0 2.5 copy.52
  201.4 1.3 multiply_reduce_fusion
  202.7 0.0 copy-start
  202.7 3.5 copy-done
  206.3 1.4 fusion
  207.6 0.0 all-gather.9.cloned.1.call-done
  207.7 30.1 %all-gather.5.cloned.1.call-done = bf16[5120,1024]{1,0:T(8,128)(2,1)} async-done(((bf16[640,1024]{1,0:T(8,128)(2,1)}), bf16[5120,1024]{1,0:T(8,128)(2,1)}) %all-gather.5.cloned.1.call-update) | async-done | bytes 10485776 | tf_op jit(solution)/shard_map/all_gather | solution.py:83
  237.8 9.8 %fusion.16 = bf16[512,1024]{1,0:T(8,128)(2,1)S(1)} fusion(bf16[5120,1024]{1,0:T(8,128)(2,1)} %all-gather.5.cloned.1.call-done, bf16[1,512,5120]{2,1,0:T(8,128)(2,1)} %all-gather.9.cloned.1.call-done), kind=kOutput, calls=%fused_computation.22 | convolution fusion | flops 5369233408 | bytes 16777216 | tf_op jit(solution)/shard_map/dot_general | solution.py:81
  247.6 0.5 copy.47
  248.2 0.0 copy-start.3
  248.2 54.7 %all-gather.7.cloned.1.call-done = bf16[5120,1024]{1,0:T(8,128)(2,1)} async-done(((bf16[640,1024]{1,0:T(8,128)(2,1)}), bf16[5120,1024]{1,0:T(8,128)(2,1)}) %all-gather.7.cloned.1.call-update) | async-done | bytes 10485776 | tf_op jit(solution)/shard_map/all_gather | solution.py:78
  302.8 9.8 %fusion.22 = bf16[64,8,8,128]{3,2,1,0:T(8,128)(2,1)S(1)} fusion(bf16[5120,1024]{1,0:T(8,128)(2,1)} %all-gather.7.cloned.1.call-done, bf16[1,512,5120]{2,1,0:T(8,128)(2,1)} %all-gather.9.cloned.1.call-done), kind=kOutput, calls=%fused_computation.24 | convolution fusion | flops 5369233408 | bytes 16777216 | tf_op jit(solution)/shard_map/dot_general | solution.py:76
  312.7 0.0 copy-done.3
  312.7 1.3 select_reduce_fusion
  314.0 0.0 slice-start
  314.0 2.4 bitcast_reduce_fusion
  316.5 0.0 slice-start.1
  316.5 2.5 fusion.12
  319.0 0.0 slice-done
  319.0 0.0 slice-done.1
  319.0 2.5 add_convert_fusion
  321.5 0.7 copy.41
  322.2 0.5 convert_element_type.54
  322.7 30.5 %all_to_all.77 = bf16[4,128,1024]{2,1,0:T(8,128)(2,1)S(1)} all-to-all(bf16[4,128,1024]{2,1,0:T(8,128)(2,1)S(1)} %convert_element_type.54), channel_id=1, replica_groups=mesh['prompt'=8,'seq'=4] {'seq'}, dimensions={0} | all-to-all | bytes 2097152 | tf_op jit(solution)/shard_map/all_to_all | solution.py:97
  353.2 0.7 copy.42
  353.9 1.3 copy.43
  (2 shorter events, 0.0 us)
Async XLA Ops:
  6.5 11.7 %copy-start.2 = (bf16[1,128,4096]{2,1,0:T(8,128)(2,1)S(1)}, bf16[1,128,4096]{2,1,0:T(8,128)(2,1)}, u32[]{:S(2)}) copy-start(bf16[1,128,4096]{2,1,0:T(8,128)(2,1)} %param.9) | copy-start | bytes 3145732
  6.5 201.1 %all-gather.9.cloned.1.call-start = ((), (), s32[]{:S(2)}) async-start(), calls=%async_computation.7 | async-start | bytes 6553600 | tf_op jit(solution)/shard_map/all_gather | solution.py:75
  7.3 230.5 %all-gather.5.cloned.1.call-start = ((), (), s32[]{:S(2)}) async-start(), calls=%async_computation.5 | async-start | bytes 11796480 | tf_op jit(solution)/shard_map/all_gather | solution.py:83
  8.0 294.8 %all-gather.7.cloned.1.call-start = ((), (), s32[]{:S(2)}) async-start(), calls=%async_computation.6 | async-start | bytes 11796480 | tf_op jit(solution)/shard_map/all_gather | solution.py:78
  11.9 61.0 %all-to-all-start = ((bf16[128,4,1024]{2,0,1:T(8,128)(2,1)}), bf16[128,4,1024]{2,0,1:T(8,128)(2,1)S(1)}, u32[]{:S(2)}, u32[]{:S(2)}) async-start(bf16[128,4,1024]{2,0,1:T(8,128)(2,1)} %copy.28), calls=%async_computation | async-start | bytes 2097152 | tf_op jit(solution)/shard_map/all_to_all | solution.py:89
  72.9 53.3 %all-to-all-start.1 = ((bf16[128,4,1024]{2,0,1:T(8,128)(2,1)}), bf16[128,4,1024]{2,0,1:T(8,128)(2,1)S(1)}, u32[]{:S(2)}, u32[]{:S(2)}) async-start(bf16[128,4,1024]{2,0,1:T(8,128)(2,1)} %copy.29), calls=%async_computation.1 | async-start | bytes 2097152 | tf_op jit(solution)/shard_map/all_to_all | solution.py:90
  126.2 45.3 %all-to-all-start.2 = ((bf16[128,4,1024]{2,0,1:T(8,128)(2,1)}), bf16[128,4,1024]{2,0,1:T(8,128)(2,1)S(1)}, u32[]{:S(2)}, u32[]{:S(2)}) async-start(bf16[128,4,1024]{2,0,1:T(8,128)(2,1)} %copy.32), calls=%async_computation.2 | async-start | bytes 2097152 | tf_op jit(solution)/shard_map/all_to_all | solution.py:91
  171.5 5.1 %copy-start.1 = (bf16[128,4,1024]{2,0,1:T(8,128)(2,1)}, bf16[128,4,1024]{2,0,1:T(8,128)(2,1)S(1)}, u32[]{:S(2)}) copy-start(bf16[128,4,1024]{2,0,1:T(8,128)(2,1)S(1)} %all-to-all-done.2) | copy-start | bytes 3145732
  171.5 27.5 %all-to-all-start.3 = ((bf16[128,4,1024]{2,0,1:T(8,128)(2,1)}), bf16[128,4,1024]{2,0,1:T(8,128)(2,1)}, u32[]{:S(2)}, u32[]{:S(2)}) async-start(bf16[128,4,1024]{2,0,1:T(8,128)(2,1)} %copy.35), calls=%async_computation.3 | async-start | bytes 2097152 | tf_op jit(solution)/shard_map/all_to_all | solution.py:92
  202.7 3.5 copy-start
  248.2 64.5 %copy-start.3 = (bf16[64,8,8,128]{3,2,1,0:T(8,128)(2,1)S(1)}, bf16[64,8,8,128]{3,2,1,0:T(8,128)(2,1)}, u32[]{:S(2)}) copy-start(bf16[64,8,8,128]{3,2,1,0:T(8,128)(2,1)} %copy.52) | copy-start | bytes 3145732
  314.0 5.0 %slice-start = ((s8[8388608]{0:T(1024)(128)(4,1)}), s8[4194304]{0:T(1024)(128)(4,1)S(1)}, s32[]{:S(2)}) async-start(s8[8388608]{0:T(1024)(128)(4,1)} %bitcast.60), calls=%async_computation.8 | async-start | bytes 8388608
  316.5 2.5 slice-start.1
Sparse Core Ops, SparseCore 0:
  8.9 164.6 all-gather.8
  175.5 62.2 all-gather.4
  239.7 63.1 all-gather.6
where the time goes:
time: 362 us
  waiting for transfers between devices  239 us (66%)
  blocking collectives  30.5 us (8%)
  matrix products  27.2 us (8%)
  local copies, waits for them, and re-layouts  25.3 us (7%)
  starting transfers between devices  21.9 us (6%)
  between operations  14 us (4%)
  other arithmetic  3.83 us (1%)
    all_gather x1, waiting for transfers between devices, body(): lax.all_gather(key_weight, 'prompt', axis=0, tiled=True)  54.7 us
    all_to_all x1, waiting for transfers between devices, body(): lax.all_to_all(query_local, 'seq', split_axis=1, concat_axis=0, tiled=True)  52.6 us
    all_to_all x1, waiting for transfers between devices, body(): lax.all_to_all(key_local, 'seq', split_axis=1, concat_axis=0, tiled=True)  46.6 us
    all_to_all x1, waiting for transfers between devices, body(): lax.all_to_all(value_local, 'seq', split_axis=1, concat_axis=0, tiled=True)  32.6 us
    all_to_all x1, blocking collectives, body(): lax.all_to_all(summed, 'seq', split_axis=0, concat_axis=1, tiled=True)  30.5 us
    all_gather x1, waiting for transfers between devices, body(): lax.all_gather(value_weight, 'prompt', axis=0, tiled=True)  30.1 us
    all_to_all x1, waiting for transfers between devices, body(): lax.all_to_all(cross_local, 'seq', split_axis=1, concat_axis=0, tiled=True)  20.3 us
    dot_general x1, matrix products, body(): jnp.dot(text_full, lax.all_gather(key_weight, 'prompt', axis=0, tiled=Tru...  9.82 us
  transfers between devices with their start and end apart: 7, of which 6 were waited for; matrix products, arithmetic and copies ran while one was open for 7% of the time, Pallas kernels for 0%

commit v1 on v0

--- a/solution.py
+++ b/solution.py
@@ -1,3 +1,4 @@
+import functools
 import math
 import jax
 import jax.numpy as jnp
@@ -5,6 +6,41 @@
 from jax.sharding import PartitionSpec as P
 
 HD = 128
+
+
+def tell_widths_all(vector, join_dim):
+    vector = jnp.moveaxis(vector, 0, join_dim)
+    base_arr = vector.shape
+    state_now = vector.reshape(
+        *base_arr[:join_dim], base_arr[join_dim] * base_arr[join_dim + 1], *base_arr[join_dim + 2 :]
+    )
+    return state_now
+
+
+def mix_paths(obj, named_axis, k_dim):
+    devs = lax.axis_size(named_axis)
+    column = [(ii, (ii + 1) % devs) for ii in range(devs)]
+    chunks = [(p, dev) for dev, p in column]
+    everything, found_now = ([], [])
+    for src_i in range(devs - 1):
+        if src_i % 2 == 0:
+            everything.append(
+                lax.ppermute(
+                    everything[-1] if everything else obj, axis_name=named_axis, perm=column
+                )
+            )
+        else:
+            found_now.append(
+                lax.ppermute(found_now[-1] if found_now else obj, axis_name=named_axis, perm=chunks)
+            )
+    taken_in = jnp.stack([*everything[::-1], obj, *found_now])
+    met_up = lax.axis_index(named_axis) - len(everything)
+    taken_in = taken_in[(jnp.arange(devs) - met_up) % devs]
+    local_now = tell_widths_all(taken_in, k_dim)
+    return local_now
+
+
+reach_the_tracks = functools.partial(mix_paths, named_axis="prompt", k_dim=0)
 
 
 def head_attend(query_rows, key_rows, value_rows, length, head_count):
@@ -79,9 +115,7 @@
         preferred_element_type=jnp.float32,
     )
     value_sums = jnp.dot(
-        text_full,
-        lax.all_gather(value_weight, "prompt", axis=0, tiled=True),
-        preferred_element_type=jnp.float32,
+        text_full, reach_the_tracks(value_weight), preferred_element_type=jnp.float32
     )
     text_keys = key_sums.astype(jnp.bfloat16)
     text_values = value_sums.astype(jnp.bfloat16)

time: 362 us -> 346 us (0.956)
  waiting for transfers between devices: 239 us -> 191 us
  local copies, waits for them, and re-layouts: 25.3 us -> 48.2 us
  starting transfers between devices: 21.9 us -> 28.2 us
    ppermute x0 -> x7, waiting for transfers between devices: none -> 72.7 us  [the longest x4 44.3 us: mix_paths(): lax.ppermute(everything[-1] if everything else obj, axis_name=named_axis,...]
    all_gather x1, waiting for transfers between devices: 54.7 us -> 0.01 us  [body(): lax.all_gather(key_weight, 'prompt', axis=0, tiled=True)]
    all_to_all x1, waiting for transfers between devices: 46.6 us -> 2.18 us  [body(): lax.all_to_all(key_local, 'seq', split_axis=1, concat_axis=0, tiled=True)]
    all_to_all x1, waiting for transfers between devices: 20.3 us -> 52.6 us  [body(): lax.all_to_all(cross_local, 'seq', split_axis=1, concat_axis=0, tiled=True)]
    all_gather x1 -> x0, waiting for transfers between devices: 30.1 us -> none  [body(): lax.all_gather(value_weight, 'prompt', axis=0, tiled=True)]
    all_to_all x1, waiting for transfers between devices: 32.6 us -> 15.3 us  [body(): lax.all_to_all(value_local, 'seq', split_axis=1, concat_axis=0, tiled=True)]
    unnamed x16 -> x23, local copies, waits for them, and re-layouts: 8.07 us -> 20.7 us
    gather x0 -> x1, local copies, waits for them, and re-layouts: none -> 9.65 us  [mix_paths(): taken_in = taken_in[(jnp.arange(devs) - met_up) % devs]]
  transfers between devices with their start and end apart: 7 -> 13, of which waited for: 6 -> 9; matrix products, arithmetic and copies ran while one was open for 7% -> 15% of each run, Pallas kernels for 0% -> 0%
where the time goes in v1:
time: 346 us; the launch traced here: 344 us
  waiting for transfers between devices  191 us (55%)
  local copies, waits for them, and re-layouts  48.2 us (14%)
  blocking collectives  30.8 us (9%)
  starting transfers between devices  28.2 us (8%)
  matrix products  28.2 us (8%)
  between operations  14.3 us (4%)
  other arithmetic  3.86 us (1%)
    all_to_all x1, waiting for transfers between devices, body(): lax.all_to_all(cross_local, 'seq', split_axis=1, concat_axis=0, tiled=True)  52.6 us
    all_to_all x1, waiting for transfers between devices, body(): lax.all_to_all(query_local, 'seq', split_axis=1, concat_axis=0, tiled=True)  46.5 us
    ppermute x4, waiting for transfers between devices, mix_paths(): lax.ppermute(everything[-1] if everything else obj, axis_name=named_axis,...  44.3 us
    all_to_all x1, blocking collectives, body(): lax.all_to_all(summed, 'seq', split_axis=0, concat_axis=1, tiled=True)  30.8 us
    ppermute x3, waiting for transfers between devices, mix_paths(): lax.ppermute(found_now[-1] if found_now else obj, axis_name=named_axis, p...  28.4 us
    unnamed x23, local copies, waits for them, and re-layouts  20.7 us
    all_to_all x1, waiting for transfers between devices, body(): lax.all_to_all(value_local, 'seq', split_axis=1, concat_axis=0, tiled=True)  15.3 us
    dot_general x1, matrix products, body(): jnp.dot(text_full, reach_the_tracks(value_weight), preferred_element_type...  10.7 us
  transfers between devices with their start and end apart: 13, of which 9 were waited for; matrix products, arithmetic and copies ran while one was open for 15% of the time, Pallas kernels for 0%

profile of v1, /device:TPU:0, one launch (start us, length us, event | category | flops | bytes accessed | tf_op | source)
XLA Modules:
  0.0 344.3 jit_solution(3895211516102057017)
XLA Ops:
  6.5 0.0 all-gather.6.cloned.1.call-start
  6.5 0.7 all-gather.6.cloned.1.call-update
  7.3 0.0 all-gather.4.cloned.1.call-start
  7.3 0.7 all-gather.4.cloned.1.call-update
  8.0 1.9 all_to_all.67
  9.9 1.3 copy.33
  11.1 6.3 %all-to-all-start.3 = ((bf16[128,4,1024]{2,0,1:T(8,128)(2,1)}), bf16[128,4,1024]{2,0,1:T(8,128)(2,1)S(1)}, u32[]{:S(2)}, u32[]{:S(2)}) async-start(bf16[128,4,1024]{2,0,1:T(8,128)(2,1)} %copy.33), calls=%async_computation.3 | async-start | bytes 2097152 | tf_op jit(solution)/shard_map/all_to_all | solution.py:126
  17.5 0.0 copy-done.1
  17.5 0.8 all_to_all.58
  18.3 1.3 copy.26
  19.6 52.6 %all-to-all-done.3 = bf16[128,4,1024]{2,0,1:T(8,128)(2,1)S(1)} async-done(((bf16[128,4,1024]{2,0,1:T(8,128)(2,1)}), bf16[128,4,1024]{2,0,1:T(8,128)(2,1)S(1)}, u32[]{:S(2)}, u32[]{:S(2)}) %all-to-all-start.3) | async-done | bytes 1048608 | tf_op jit(solution)/shard_map/all_to_all | solution.py:126
  72.2 3.5 %all-to-all-start = ((bf16[128,4,1024]{2,0,1:T(8,128)(2,1)}), bf16[128,4,1024]{2,0,1:T(8,128)(2,1)S(1)}, u32[]{:S(2)}, u32[]{:S(2)}) async-start(bf16[128,4,1024]{2,0,1:T(8,128)(2,1)} %copy.26), calls=%async_computation | async-start | bytes 2097152 | tf_op jit(solution)/shard_map/all_to_all | solution.py:123
  75.7 0.1 collective-permute-start
  75.8 1.9 all_to_all.61
  77.6 1.3 copy.27
  78.9 46.5 %all-to-all-done = bf16[128,4,1024]{2,0,1:T(8,128)(2,1)S(1)} async-done(((bf16[128,4,1024]{2,0,1:T(8,128)(2,1)}), bf16[128,4,1024]{2,0,1:T(8,128)(2,1)S(1)}, u32[]{:S(2)}, u32[]{:S(2)}) %all-to-all-start) | async-done | bytes 1048608 | tf_op jit(solution)/shard_map/all_to_all | solution.py:123
  125.5 7.5 %all-to-all-start.1 = ((bf16[128,4,1024]{2,0,1:T(8,128)(2,1)}), bf16[128,4,1024]{2,0,1:T(8,128)(2,1)S(1)}, u32[]{:S(2)}, u32[]{:S(2)}) async-start(bf16[128,4,1024]{2,0,1:T(8,128)(2,1)} %copy.27), calls=%async_computation.1 | async-start | bytes 2097152 | tf_op jit(solution)/shard_map/all_to_all | solution.py:124
  133.0 0.0 collective-permute-done
  133.0 0.0 collective-permute-start.1
  133.0 2.6 collective-permute-start.4
  135.6 27.8 %collective-permute-done.1 = bf16[640,1024]{1,0:T(8,128)(2,1)} collective-permute-done((bf16[640,1024]{1,0:T(8,128)(2,1)}, bf16[640,1024]{1,0:T(8,128)(2,1)}, u32[]{:S(2)}, u32[]{:S(2)}) %collective-permute-start.1) | collective-permute-done | bytes 1310752 | tf_op jit(solution)/shard_map/ppermute | solution.py:28
  163.4 0.0 collective-permute-start.2
  163.4 2.6 all_to_all.64
  166.1 2.5 copy.30
  168.6 2.2 all-to-all-done.1
  170.7 4.2 %all-to-all-start.2 = ((bf16[128,4,1024]{2,0,1:T(8,128)(2,1)}), bf16[128,4,1024]{2,0,1:T(8,128)(2,1)}, u32[]{:S(2)}, u32[]{:S(2)}) async-start(bf16[128,4,1024]{2,0,1:T(8,128)(2,1)} %copy.30), calls=%async_computation.2 | async-start | bytes 2097152 | tf_op jit(solution)/shard_map/all_to_all | solution.py:125
  175.7 0.0 collective-permute-done.4
  175.7 1.1 collective-permute-start.5
  176.7 6.6 %collective-permute-done.2 = bf16[640,1024]{1,0:T(8,128)(2,1)} collective-permute-done((bf16[640,1024]{1,0:T(8,128)(2,1)}, bf16[640,1024]{1,0:T(8,128)(2,1)}, u32[]{:S(2)}, u32[]{:S(2)}) %collective-permute-start.2) | collective-permute-done | bytes 1310752 | tf_op jit(solution)/shard_map/ppermute | solution.py:28
  183.3 0.0 collective-permute-start.3
  183.4 1.2 copy.48
  184.6 0.3 copy.45
  184.9 0.3 copy.46
  185.2 15.3 %all-to-all-done.2 = bf16[128,4,1024]{2,0,1:T(8,128)(2,1)} async-done(((bf16[128,4,1024]{2,0,1:T(8,128)(2,1)}), bf16[128,4,1024]{2,0,1:T(8,128)(2,1)}, u32[]{:S(2)}, u32[]{:S(2)}) %all-to-all-start.2) | async-done | bytes 1048608 | tf_op jit(solution)/shard_map/all_to_all | solution.py:125
  200.5 1.5 copy.47
  202.0 1.3 multiply_reduce_fusion
  203.3 1.4 fusion
  204.6 12.7 %collective-permute-done.5 = bf16[640,1024]{1,0:T(8,128)(2,1)} collective-permute-done((bf16[640,1024]{1,0:T(8,128)(2,1)}, bf16[640,1024]{1,0:T(8,128)(2,1)}, u32[]{:S(2)}, u32[]{:S(2)}) %collective-permute-start.5) | collective-permute-done | bytes 1310752 | tf_op jit(solution)/shard_map/ppermute | solution.py:34
  217.4 2.8 collective-permute-start.6
  220.2 9.9 %collective-permute-done.3 = bf16[640,1024]{1,0:T(8,128)(2,1)} collective-permute-done((bf16[640,1024]{1,0:T(8,128)(2,1)}, bf16[640,1024]{1,0:T(8,128)(2,1)}, u32[]{:S(2)}, u32[]{:S(2)}) %collective-permute-start.3) | collective-permute-done | bytes 1310752 | tf_op jit(solution)/shard_map/ppermute | solution.py:28
  230.1 2.5 bitcast_dynamic-update-slice_fusion.7
  232.6 2.5 bitcast_dynamic-update-slice_fusion.6
  235.1 2.5 bitcast_dynamic-update-slice_fusion.5
  237.6 2.5 bitcast_dynamic-update-slice_fusion.4
  240.1 0.0 copy-done
  240.1 2.5 bitcast_dynamic-update-slice_fusion.3
  242.6 2.5 bitcast_dynamic-update-slice_fusion.2
  245.1 2.5 bitcast_dynamic-update-slice_fusion.1
  247.6 15.7 %collective-permute-done.6 = bf16[640,1024]{1,0:T(8,128)(2,1)S(1)} collective-permute-done((bf16[640,1024]{1,0:T(8,128)(2,1)}, bf16[640,1024]{1,0:T(8,128)(2,1)S(1)}, u32[]{:S(2)}, u32[]{:S(2)}) %collective-permute-start.6) | collective-permute-done | bytes 1310752 | tf_op jit(solution)/shard_map/ppermute | solution.py:34
  263.3 1.2 bitcast_dynamic-update-slice_fusion
  264.4 9.7 %gather_fusion = bf16[8,640,1024]{2,1,0:T(8,128)(2,1)} fusion(bf16[8,640,1024]{2,1,0:T(8,128)(2,1)} %bitcast_dynamic-update-slice_fusion, s32[1024]{0:T(1024)S(1)} %pad_clamp_fusion), kind=kCustom, calls=%fused_computation | custom fusion | bytes 20971552 | tf_op jit(solution)/shard_map/gather | solution.py:38
  274.1 10.7 %fusion.19 = bf16[1024,512]{1,0:T(8,128)(2,1)} fusion(bf16[5120,1024]{1,0:T(8,128)(2,1)} %bitcast.83, bf16[1,512,5120]{2,1,0:T(8,128)(2,1)} %all-gather.6.cloned.1.call-done), kind=kOutput, calls=%fused_computation.24 | convolution fusion | flops 5369233408 | bytes 16777216 | tf_op jit(solution)/shard_map/dot_general | solution.py:117
  284.8 9.9 %fusion.22 = bf16[64,8,8,128]{3,2,1,0:T(8,128)(2,1)S(1)} fusion(bf16[5120,1024]{1,0:T(8,128)(2,1)} %all-gather.4.cloned.1.call-done, bf16[1,512,5120]{2,1,0:T(8,128)(2,1)} %all-gather.6.cloned.1.call-done), kind=kOutput, calls=%fused_computation.25 | convolution fusion | flops 5369233408 | bytes 16777216 | tf_op jit(solution)/shard_map/dot_general | solution.py:112
  294.7 0.0 copy-start.3
  294.7 1.4 select_reduce_fusion
  296.1 2.4 bitcast_reduce_fusion
  298.6 0.0 slice-start.1
  298.6 2.5 fusion.12
  301.1 2.5 add_convert_fusion
  303.6 0.7 copy.38
  304.2 0.5 convert_element_type.58
  304.7 30.8 %all_to_all.77 = bf16[4,128,1024]{2,1,0:T(8,128)(2,1)S(1)} all-to-all(bf16[4,128,1024]{2,1,0:T(8,128)(2,1)S(1)} %convert_element_type.58), channel_id=1, replica_groups=mesh['prompt'=8,'seq'=4] {'seq'}, dimensions={0} | all-to-all | bytes 2097152 | tf_op jit(solution)/shard_map/all_to_all | solution.py:131
  335.5 0.7 copy.39
  336.2 1.3 copy.40
  (14 shorter events, 0.0 us)
Async XLA Ops:
  6.5 11.0 %copy-start.1 = (bf16[1,128,4096]{2,1,0:T(8,128)(2,1)S(1)}, bf16[1,128,4096]{2,1,0:T(8,128)(2,1)}, u32[]{:S(2)}) copy-start(bf16[1,128,4096]{2,1,0:T(8,128)(2,1)} %param.8) | copy-start | bytes 3145732
  6.5 267.5 %all-gather.6.cloned.1.call-start = ((), (), s32[]{:S(2)}) async-start(), calls=%async_computation.6 | async-start | bytes 6553600 | tf_op jit(solution)/shard_map/all_gather | solution.py:111
  7.3 277.5 %all-gather.4.cloned.1.call-start = ((), (), s32[]{:S(2)}) async-start(), calls=%async_computation.5 | async-start | bytes 11796480 | tf_op jit(solution)/shard_map/all_gather | solution.py:114
  11.1 61.0 %all-to-all-start.3 = ((bf16[128,4,1024]{2,0,1:T(8,128)(2,1)}), bf16[128,4,1024]{2,0,1:T(8,128)(2,1)S(1)}, u32[]{:S(2)}, u32[]{:S(2)}) async-start(bf16[128,4,1024]{2,0,1:T(8,128)(2,1)} %copy.33), calls=%async_computation.3 | async-start | bytes 2097152 | tf_op jit(solution)/shard_map/all_to_all | solution.py:126
  72.2 53.3 %all-to-all-start = ((bf16[128,4,1024]{2,0,1:T(8,128)(2,1)}), bf16[128,4,1024]{2,0,1:T(8,128)(2,1)S(1)}, u32[]{:S(2)}, u32[]{:S(2)}) async-start(bf16[128,4,1024]{2,0,1:T(8,128)(2,1)} %copy.26), calls=%async_computation | async-start | bytes 2097152 | tf_op jit(solution)/shard_map/all_to_all | solution.py:123
  75.7 57.3 %collective-permute-start = (bf16[640,1024]{1,0:T(8,128)(2,1)}, bf16[640,1024]{1,0:T(8,128)(2,1)}, u32[]{:S(2)}, u32[]{:S(2)}) collective-permute-start(bf16[640,1024]{1,0:T(8,128)(2,1)} %param.14), channel_id=1, source_target_pairs={{0,4},{4,8},{8,12},{12,16},{16,20},{20,24},{24,28},{28,0},{1,5},{5... | collective-permute-start | bytes 3932168 | tf_op jit(solution)/shard_map/ppermute | solution.py:28
  125.5 45.3 %all-to-all-start.1 = ((bf16[128,4,1024]{2,0,1:T(8,128)(2,1)}), bf16[128,4,1024]{2,0,1:T(8,128)(2,1)S(1)}, u32[]{:S(2)}, u32[]{:S(2)}) async-start(bf16[128,4,1024]{2,0,1:T(8,128)(2,1)} %copy.27), calls=%async_computation.1 | async-start | bytes 2097152 | tf_op jit(solution)/shard_map/all_to_all | solution.py:124
  133.0 30.4 %collective-permute-start.1 = (bf16[640,1024]{1,0:T(8,128)(2,1)}, bf16[640,1024]{1,0:T(8,128)(2,1)}, u32[]{:S(2)}, u32[]{:S(2)}) collective-permute-start(bf16[640,1024]{1,0:T(8,128)(2,1)} %collective-permute-done), channel_id=1, source_target_pairs={{0,4},{4,8},{8,12},{12,16},{16,20},{20,24},{24,28},{28,0},{1,5},{5... | collective-permute-start | bytes 3932168 | tf_op jit(solution)/shard_map/ppermute | solution.py:28
  133.0 42.7 %collective-permute-start.4 = (bf16[640,1024]{1,0:T(8,128)(2,1)}, bf16[640,1024]{1,0:T(8,128)(2,1)}, u32[]{:S(2)}, u32[]{:S(2)}) collective-permute-start(bf16[640,1024]{1,0:T(8,128)(2,1)} %param.14), channel_id=1, source_target_pairs={{4,0},{8,4},{12,8},{16,12},{20,16},{24,20},{28,24},{0,28},{5,1},{9... | collective-permute-start | bytes 3932168 | tf_op jit(solution)/shard_map/ppermute | solution.py:34
  163.4 19.9 %collective-permute-start.2 = (bf16[640,1024]{1,0:T(8,128)(2,1)}, bf16[640,1024]{1,0:T(8,128)(2,1)}, u32[]{:S(2)}, u32[]{:S(2)}) collective-permute-start(bf16[640,1024]{1,0:T(8,128)(2,1)} %collective-permute-done.1), channel_id=1, source_target_pairs={{0,4},{4,8},{8,12},{12,16},{16,20},{20,24},{24,28},{28,0},{1,5},{5... | collective-permute-start | bytes 3932168 | tf_op jit(solution)/shard_map/ppermute | solution.py:28
  170.7 29.7 %all-to-all-start.2 = ((bf16[128,4,1024]{2,0,1:T(8,128)(2,1)}), bf16[128,4,1024]{2,0,1:T(8,128)(2,1)}, u32[]{:S(2)}, u32[]{:S(2)}) async-start(bf16[128,4,1024]{2,0,1:T(8,128)(2,1)} %copy.30), calls=%async_computation.2 | async-start | bytes 2097152 | tf_op jit(solution)/shard_map/all_to_all | solution.py:125
  175.7 41.7 %collective-permute-start.5 = (bf16[640,1024]{1,0:T(8,128)(2,1)}, bf16[640,1024]{1,0:T(8,128)(2,1)}, u32[]{:S(2)}, u32[]{:S(2)}) collective-permute-start(bf16[640,1024]{1,0:T(8,128)(2,1)} %collective-permute-done.4), channel_id=1, source_target_pairs={{4,0},{8,4},{12,8},{16,12},{20,16},{24,20},{28,24},{0,28},{5,1},{9... | collective-permute-start | bytes 3932168 | tf_op jit(solution)/shard_map/ppermute | solution.py:34
  183.3 46.8 %collective-permute-start.3 = (bf16[640,1024]{1,0:T(8,128)(2,1)}, bf16[640,1024]{1,0:T(8,128)(2,1)}, u32[]{:S(2)}, u32[]{:S(2)}) collective-permute-start(bf16[640,1024]{1,0:T(8,128)(2,1)} %collective-permute-done.2), channel_id=1, source_target_pairs={{0,4},{4,8},{8,12},{12,16},{16,20},{20,24},{24,28},{28,0},{1,5},{5... | collective-permute-start | bytes 3932168 | tf_op jit(solution)/shard_map/ppermute | solution.py:28
  203.2 36.8 %copy-start = (f32[8,512,512]{1,2,0:T(8,128)}, f32[8,512,512]{1,2,0:T(8,128)S(1)}, u32[]{:S(2)}) copy-start(f32[8,512,512]{1,2,0:T(8,128)S(1)} %get-tuple-element.33) | copy-start | bytes 25165828
  217.4 45.9 %collective-permute-start.6 = (bf16[640,1024]{1,0:T(8,128)(2,1)}, bf16[640,1024]{1,0:T(8,128)(2,1)S(1)}, u32[]{:S(2)}, u32[]{:S(2)}) collective-permute-start(bf16[640,1024]{1,0:T(8,128)(2,1)} %collective-permute-done.5), channel_id=1, source_target_pairs={{4,0},{8,4},{12,8},{16,12},{20,16},{24,20},{28,24},{0,28},{5,1},{9... | collective-permute-start | bytes 3932168 | tf_op jit(solution)/shard_map/ppermute | solution.py:34
  284.8 9.9 %copy-start.2 = (bf16[64,8,8,128]{3,2,1,0:T(8,128)(2,1)S(1)}, bf16[64,8,8,128]{3,2,1,0:T(8,128)(2,1)}, u32[]{:S(2)}) copy-start(bf16[64,8,8,128]{3,2,1,0:T(8,128)(2,1)} %copy.48) | copy-start | bytes 3145732
  294.7 3.8 %copy-start.3 = (bf16[1024,512]{1,0:T(8,128)(2,1)S(1)}, bf16[1024,512]{1,0:T(8,128)(2,1)}, u32[]{:S(2)}) copy-start(bf16[1024,512]{1,0:T(8,128)(2,1)} %fusion.19) | copy-start | bytes 3145732
  296.1 5.0 %slice-start = ((s8[8388608]{0:T(1024)(128)(4,1)}), s8[4194304]{0:T(1024)(128)(4,1)S(1)}, s32[]{:S(2)}) async-start(s8[8388608]{0:T(1024)(128)(4,1)} %bitcast.81), calls=%async_computation.7 | async-start | bytes 8388608
  298.6 2.5 slice-start.1
Sparse Core Ops, SparseCore 0:
  8.9 163.9 all-gather.5
  174.8 92.8 all-gather.3
